TPU v7x, 32 devices: a whole 2x2x4 slice. The times are simulated.
32 devices in a mesh: dp: 2 (over y), seq: 4 (over z), tensor: 4 (over x, core).
Axes of the slice: x: 2, y: 2, z: 4, core: 2. Of those that a mesh axis runs over, the one named last changes fastest.
Arguments:
- layer_input: bfloat16 [6, 1024, 2048], P('dp', 'seq'), may hold values from -6 to 6
- lengths: int32 [6], P('dp'), may hold values from 256 to 1024, as said below
- cotangent: bfloat16 [6, 1024, 2048], P('dp', ('seq', 'tensor')), may hold values from -6 to 6
- ln1_gain: bfloat16 [2048], replicated, may hold values from 0.5 to 1.5
- ln1_bias: bfloat16 [2048], replicated, may hold values from -3 to 3
- w_query: bfloat16 [2048, 2048], P(None, 'tensor'), may hold values from -0.125 to 0.125
- b_query: bfloat16 [2048], P('tensor'), may hold values from -3 to 3
- w_kv: bfloat16 [2048, 256], replicated, may hold values from -0.125 to 0.125
- b_value: bfloat16 [128], replicated, may hold values from -3 to 3
- w_out: bfloat16 [2048, 2048], P('tensor'), may hold values from -0.5 to 0.5
- b_out: bfloat16 [2048], replicated, may hold values from -3 to 3
- ln2_gain: bfloat16 [2048], replicated, may hold values from 0.5 to 1.5
- ln2_bias: bfloat16 [2048], replicated, may hold values from -3 to 3
- w_up: bfloat16 [2048, 8192], P(None, 'tensor'), may hold values from -0.125 to 0.125
- b_up: bfloat16 [8192], P('tensor'), may hold values from -3 to 3
- w_down: bfloat16 [8192, 2048], P('tensor'), may hold values from -0.0625 to 0.0625
- b_down: bfloat16 [2048], replicated, may hold values from -3 to 3
Outputs:
- layer_output: bfloat16 [6, 1024, 2048], P('dp', ('seq', 'tensor'))
- input_grad: float32 [6, 1024, 2048], P('dp', ('seq', 'tensor'))
- g_w_query: float32 [2048, 2048], P(('dp', 'seq'), 'tensor')
- g_b_query: float32 [16, 128], P('tensor', ('dp', 'seq'))
- g_w_kv: float32 [2048, 256], P(('dp', 'seq', 'tensor'))
- g_b_value: float32 [128], P(('dp', 'seq', 'tensor'))
- g_w_out: float32 [2048, 2048], P('tensor', ('dp', 'seq'))
- g_w_up: float32 [2048, 8192], P(('dp', 'seq'), 'tensor')
- g_b_up: float32 [64, 128], P('tensor', ('dp', 'seq'))
- g_w_down: float32 [8192, 2048], P('tensor', ('dp', 'seq'))
- g_norms_biases: float32 [6, 2048], P(None, ('dp', 'seq', 'tensor'))
Inputs may be any that keep to these rules, and one draw needn't show every extreme that they name: `lengths`: the number of real tokens at the start of each row; the rest of the row is padding.
All inputs are finite; a program needn't handle non-finite values.
Results may differ from a plain program's by a relative error of at most 0.012.
Values may be sent and summed in bfloat16 or wider, within the bound.
A program may use at most 256 MiB of HBM per device.

v0:
```python
import math
import jax
import jax.numpy as jnp
from jax import lax
from jax.sharding import PartitionSpec as P

NORM_EPS = 1e-05
BF16 = jnp.bfloat16
F32 = jnp.float32


def normalize(values_in):
    row_mean = jnp.mean(values_in, -1, keepdims=True)
    centered = values_in - row_mean
    variance = jnp.mean(centered * centered, -1, keepdims=True)
    inv_std = lax.rsqrt(variance + NORM_EPS)
    return (centered * inv_std, inv_std)


def norm_back(grad_in, normed, inv_std, norm_gain):
    scaled = grad_in * norm_gain
    mean_scaled = jnp.mean(scaled, -1, keepdims=True)
    mean_mixed = jnp.mean(scaled * normed, -1, keepdims=True)
    return inv_std * (scaled - mean_scaled - normed * mean_mixed)


def across_rows(left_in, right_in):
    return lax.dot_general(left_in, right_in, (((0,), (0,)), ((), ())), preferred_element_type=F32)


def times_transposed(left_in, right_in):
    return lax.dot_general(left_in, right_in, (((1,), (1,)), ((), ())), preferred_element_type=F32)


def dp_exchange(part_for):
    n_dp = lax.axis_size("dp")
    me = lax.axis_index("dp")
    arrived = []
    for k in range(1, n_dp):
        target = lax.rem(me + k, n_dp)
        pairs = [(i, (i + k) % n_dp) for i in range(n_dp)]
        arrived.append(lax.ppermute(part_for(target).astype(BF16), "dp", pairs))
    total = part_for(me)
    for piece in arrived:
        total = total + piece.astype(F32)
    return total


def two_stage(part_for, dim):
    total = dp_exchange(part_for)
    return lax.psum_scatter(total.astype(BF16), "seq", scatter_dimension=dim, tiled=True).astype(
        F32
    )


def shards(
    layer_input,
    lengths,
    cotangent,
    ln1_gain,
    ln1_bias,
    w_query,
    b_query,
    w_kv,
    b_value,
    w_out,
    b_out,
    ln2_gain,
    ln2_bias,
    w_up,
    b_up,
    w_down,
    b_down,
):
    n_rows, seq_len, model_width = layer_input.shape
    n_tensor = lax.axis_size("tensor")
    n_dp = lax.axis_size("dp")
    n_seq = lax.axis_size("seq")
    share_len = seq_len // n_tensor
    tensor_index = lax.axis_index("tensor")
    seq_index = lax.axis_index("seq")
    full_len = seq_len * n_seq
    head_size = w_kv.shape[1] // 2
    num_heads = w_query.shape[1] // head_size
    q_scale = 1.0 / math.sqrt(head_size)
    n_tok = n_rows * seq_len
    n_own = n_rows * share_len

    def own_rows(values_in):
        return lax.dynamic_slice_in_dim(values_in, tensor_index * share_len, share_len, 1)

    def gather_own(values_in):
        return lax.all_gather(values_in, "tensor", axis=1, tiled=True)

    def scatter_own(values_in):
        return lax.psum_scatter(
            values_in.astype(BF16).reshape(n_rows, seq_len, model_width),
            "tensor",
            scatter_dimension=1,
            tiled=True,
        ).astype(F32)

    positions = seq_index * seq_len + jnp.arange(seq_len, dtype=jnp.int32)
    key_places = jnp.arange(full_len, dtype=jnp.int32)
    is_valid = (positions[None, :] < lengths[:, None]).astype(F32)
    allowed_keys = (key_places[None, None, :] <= positions[None, :, None]) & (
        key_places[None, None, :] < lengths[:, None, None]
    )
    valid_own = own_rows(is_valid)
    x_float = layer_input.astype(F32)
    normed_x1, inv_one = normalize(x_float)
    normed_one = (normed_x1 * ln1_gain + ln1_bias).astype(BF16)
    flat_one = normed_one.reshape(n_tok, model_width)
    kv_bias = jnp.concatenate([jnp.zeros((head_size,), F32), b_value.astype(F32)])
    kv_local = (jnp.dot(flat_one, w_kv, preferred_element_type=F32) + kv_bias).astype(BF16)
    kv_local = kv_local.reshape(n_rows, seq_len, 2 * head_size)
    kv_all = lax.all_gather(kv_local, "seq", axis=1, tiled=True)
    queries = ((jnp.dot(flat_one, w_query, preferred_element_type=F32) + b_query) * q_scale).astype(
        BF16
    )
    queries = queries.reshape(n_rows, seq_len, num_heads, head_size)
    key_rows = kv_all[..., :head_size]
    value_rows = kv_all[..., head_size:]
    grad_y_own = cotangent.astype(F32) * valid_own[..., None]
    grad_y_low = gather_own(grad_y_own.astype(BF16)).reshape(n_tok, model_width)

    def scores_of(query_rows):
        raw_scores = jnp.einsum("rshd,rld->rhsl", query_rows, key_rows, preferred_element_type=F32)
        return jnp.where(allowed_keys[:, None], raw_scores, -1e30)

    scores = scores_of(queries)
    row_max = jnp.max(scores, -1, keepdims=True)
    exp_scores = jnp.exp(scores - row_max)
    exp_total = jnp.sum(exp_scores, -1, keepdims=True)
    soft_probs = exp_scores / exp_total
    log_total = row_max + jnp.log(exp_total)
    mixed_heads = jnp.einsum(
        "rhsl,rld->rshd", soft_probs.astype(BF16), value_rows, preferred_element_type=F32
    ).astype(BF16)
    mixed_heads = mixed_heads.reshape(n_tok, num_heads * head_size)
    attn_own = scatter_own(jnp.dot(mixed_heads, w_out, preferred_element_type=F32))
    x_own = own_rows(x_float)
    resid_own = x_own + (attn_own + b_out)
    normed_x2, inv_two = normalize(resid_own)
    normed_two = (normed_x2 * ln2_gain + ln2_bias).astype(BF16)
    flat_two = gather_own(normed_two).reshape(n_tok, model_width)
    pre_act = jnp.dot(flat_two, w_up, preferred_element_type=F32) + b_up
    activated, gelu_pull = jax.vjp(
        lambda inner_in: jax.nn.gelu(inner_in, approximate=True), pre_act
    )
    act_low = activated.astype(BF16)
    grad_act = times_transposed(grad_y_low, w_down)
    grad_pre = gelu_pull(grad_act)[0].astype(BF16)
    half_width = model_width // n_dp

    def columns(values_in, d):
        return lax.dynamic_slice_in_dim(values_in, d * half_width, half_width, 1)

    grad_n2 = scatter_own(times_transposed(grad_pre, w_up))
    g_w_down = two_stage(lambda d: across_rows(act_low, columns(grad_y_low, d)), 1)
    g_w_up = two_stage(lambda d: across_rows(columns(flat_two, d), grad_pre), 0)
    g_b_up = jnp.sum(grad_pre.astype(F32), axis=0)
    mlp_own = scatter_own(jnp.dot(act_low, w_down, preferred_element_type=F32)) + b_down
    y_own = (valid_own[..., None] * (resid_own + mlp_own)).astype(BF16)
    grad_resid = grad_y_own + norm_back(grad_n2, normed_x2, inv_two, ln2_gain)
    grad_resid_low = grad_resid.astype(BF16)
    flat_resid = gather_own(grad_resid_low).reshape(n_tok, model_width)
    g_ln2_gain = jnp.sum(grad_n2 * normed_x2, axis=(0, 1))
    g_ln2_bias = jnp.sum(grad_n2, axis=(0, 1))
    g_b_out = jnp.sum(grad_resid_low.astype(F32), axis=(0, 1))
    g_b_down = jnp.sum(grad_y_own, axis=(0, 1))
    g_w_out = two_stage(lambda d: across_rows(mixed_heads, columns(flat_resid, d)), 1)
    grad_mixed = times_transposed(flat_resid, w_out).astype(BF16)
    grad_mixed = grad_mixed.reshape(n_rows, seq_len, num_heads, head_size)
    again_probs = jnp.exp(scores_of(queries) - log_total)
    grad_probs = jnp.einsum("rshd,rld->rhsl", grad_mixed, value_rows, preferred_element_type=F32)
    inner_sum = jnp.sum(again_probs * grad_probs, -1, keepdims=True)
    grad_scores = (again_probs * (grad_probs - inner_sum)).astype(BF16)
    grad_query = jnp.einsum(
        "rhsl,rld->rshd", grad_scores, key_rows, preferred_element_type=F32
    ).astype(BF16)
    grad_keys = jnp.einsum("rhsl,rshd->rld", grad_scores, queries, preferred_element_type=F32)
    grad_values = jnp.einsum(
        "rhsl,rshd->rld", again_probs.astype(BF16), grad_mixed, preferred_element_type=F32
    )
    grad_kv = jnp.concatenate([grad_keys, grad_values], -1)
    grad_kv_own = lax.psum_scatter(grad_kv.astype(BF16), "seq", scatter_dimension=1, tiled=True)
    grad_kv_own = lax.psum_scatter(grad_kv_own, "tensor", scatter_dimension=1, tiled=True)
    flat_query = grad_query.reshape(n_tok, num_heads * head_size)
    g_b_query = jnp.sum(flat_query.astype(F32), axis=0) * q_scale
    grad_n1 = scatter_own(times_transposed(flat_query, w_query) * q_scale)
    g_w_query = two_stage(lambda d: across_rows(columns(flat_one, d), flat_query) * q_scale, 0)
    flat_kv = grad_kv_own.reshape(n_own, 2 * head_size)
    grad_n1 = grad_n1 + times_transposed(flat_kv, w_kv).reshape(n_rows, share_len, model_width)
    one_own = own_rows(normed_one).reshape(n_own, model_width)
    g_w_kv = across_rows(one_own, flat_kv)
    g_b_value = jnp.sum(flat_kv[:, head_size:].astype(F32), axis=0)
    normed_x1_own = own_rows(normed_x1)
    x_grad_own = grad_resid + norm_back(grad_n1, normed_x1_own, own_rows(inv_one), ln1_gain)
    g_ln1_gain = jnp.sum(grad_n1 * normed_x1_own, axis=(0, 1))
    g_ln1_bias = jnp.sum(grad_n1, axis=(0, 1))
    owners = n_dp * n_seq
    small = jnp.stack([g_ln1_gain, g_ln1_bias, g_ln2_gain, g_ln2_bias, g_b_out, g_b_down])
    kv_piece = g_w_kv.reshape(owners, n_tensor, -1)
    small_width = model_width // (owners * n_tensor)
    small_piece = jnp.moveaxis(small.reshape(6, owners, n_tensor, small_width), 0, 2).reshape(
        owners, n_tensor, -1
    )
    value_piece = g_b_value.reshape(owners, n_tensor, -1)
    packed = jnp.concatenate([kv_piece, small_piece, value_piece], -1)
    packed = lax.psum_scatter(
        packed.astype(BF16), "tensor", scatter_dimension=1, tiled=True
    ).astype(F32)[:, 0]
    query_table = jnp.moveaxis(g_b_query.reshape(num_heads, owners, -1), 1, 0).reshape(owners, -1)
    up_table = jnp.moveaxis(g_b_up.reshape(-1, owners, 128 // owners), 1, 0).reshape(owners, -1)
    packed = jnp.concatenate([packed, query_table, up_table], -1)
    packed = lax.psum_scatter(
        packed.astype(BF16), ("dp", "seq"), scatter_dimension=0, tiled=True
    ).astype(F32)[0]
    sizes = [
        kv_piece.shape[-1],
        small_piece.shape[-1],
        value_piece.shape[-1],
        query_table.shape[-1],
        up_table.shape[-1],
    ]
    ends = [sum(sizes[: i + 1]) for i in range(len(sizes))]
    kv_out, small_out, value_out, query_out, up_out = [
        packed[e - s : e] for s, e in zip(sizes, ends)
    ]
    return (
        y_own,
        x_grad_own,
        g_w_query,
        query_out.reshape(num_heads, -1),
        kv_out.reshape(-1, 2 * head_size),
        value_out,
        g_w_out,
        g_w_up,
        up_out.reshape(-1, 128 // owners),
        g_w_down,
        small_out.reshape(6, -1),
    )


def solution(mesh):
    placed = (
        P("dp", "seq", None),
        P("dp"),
        P("dp", ("seq", "tensor"), None),
        P(),
        P(),
        P(None, "tensor"),
        P("tensor"),
        P(),
        P(),
        P("tensor", None),
        P(),
        P(),
        P(),
        P(None, "tensor"),
        P("tensor"),
        P("tensor", None),
        P(),
    )
    return jax.shard_map(
        shards,
        mesh=mesh,
        in_specs=placed,
        out_specs=(
            P("dp", ("seq", "tensor"), None),
            P("dp", ("seq", "tensor"), None),
            P(("dp", "seq"), "tensor"),
            P("tensor", ("dp", "seq")),
            P(("dp", "seq", "tensor"), None),
            P(("dp", "seq", "tensor")),
            P("tensor", ("dp", "seq")),
            P(("dp", "seq"), "tensor"),
            P("tensor", ("dp", "seq")),
            P("tensor", ("dp", "seq")),
            P(None, ("dp", "seq", "tensor")),
        ),
        check_vma=False,
    )
```

profile of v0, /device:TPU:0, one launch (start us, length us, event | category | flops | bytes accessed | tf_op | source)
XLA Modules:
  0.0 808.1 jit_solution(13666337548137846042)
XLA Ops:
  17.0 5.2 multiply_convert_fusion.4
  26.1 30.3 %all-gather.5.cloned.1.call-done = bf16[3,1024,256]{2,1,0:T(8,128)(2,1)} async-done(((bf16[3,256,256]{2,1,0:T(8,128)(2,1)}), bf16[3,1024,256]{2,1,0:T(8,128)(2,1)}) %all-gather.5.cloned.1.call-update) | async-done | bytes 1572880 | tf_op jit(solution)/shard_map/all_gather | solution.py:117
  56.4 7.7 fusion.4
  64.1 7.0 fusion.3
  71.1 7.3 fusion.55
  85.3 5.4 convert_element_type.180
  90.7 31.2 %reduce-scatter.11.cloned.1.call-done = bf16[3,64,2048]{2,1,0:T(8,128)(2,1)} async-done(((bf16[3,256,2048]{2,1,0:T(8,128)(2,1)}), bf16[3,64,2048]{2,1,0:T(8,128)(2,1)}) %reduce-scatter.11.cloned.1.call-update) | async-done | bytes 786448 | tf_op jit(solution)/shard_map/reduce_scatter | solution.py:96
  129.0 26.0 %all-gather.7.cloned.1.call-done = bf16[3,256,2048]{2,1,0:T(8,128)(2,1)} async-done(((bf16[3,64,2048]{2,1,0:T(8,128)(2,1)}), bf16[3,256,2048]{2,1,0:T(8,128)(2,1)}) %all-gather.7.cloned.1.call-update) | async-done | bytes 3145744 | tf_op jit(solution)/shard_map/all_gather | solution.py:93
  155.0 14.2 %multiply_convert_fusion.1 = (bf16[768,2048]{1,0:T(8,128)(2,1)}, f32[768,2048]{1,0:T(8,128)}) fusion(f32[2048]{0:T(1024)S(1)} %convert_element_type.196, bf16[768,2048]{1,0:T(8,128)(2,1)} %bitcast.168, bf16[2048,2048]{1,0:T(8,128)(2,1)} %param.30), kind=kOutput, calls=%fused_computation.26 | convolution fusion | flops 6458179584 | bytes 20979712 | tf_op jit(solution)/shard_map/dot_general | solution.py:147
  169.2 16.3 %all-gather.9.cloned.1.call-done = bf16[3,256,2048]{2,1,0:T(8,128)(2,1)} async-done(((bf16[3,64,2048]{2,1,0:T(8,128)(2,1)}), bf16[3,256,2048]{2,1,0:T(8,128)(2,1)}) %all-gather.9.cloned.1.call-update) | async-done | bytes 3145744 | tf_op jit(solution)/shard_map/all_gather | solution.py:93
  185.5 14.7 %fusion.85 = (bf16[2048]{0:T(1024)(128)(2,1)S(1)}, bf16[768,2048]{1,0:T(8,128)(2,1)S(1)}) fusion(f32[768,2048]{1,0:T(8,128)} %get-tuple-element.36, f32[2048]{0:T(1024)S(1)} %convert_element_type.196, bf16[768,2048]{1,0:T(8,128)(2,1)} %bitcast.165, bf16[2048,2048]{1,0:T(8,128)(2,1)} %param.32), kind=kOutput, calls=%fused_computation.154 | convolution fusion | flops 6477051904 | bytes 20983808 | tf_op jit(solution)/shard_map/dot_general | solution.py:32
  200.2 11.5 %convolution_convert_fusion.2 = bf16[768,2048]{1,0:T(8,128)(2,1)} fusion(bf16[768,2048]{1,0:T(8,128)(2,1)S(1)} %get-tuple-element.19, bf16[2048,2048]{1,0:T(8,128)(2,1)} %param.30), kind=kOutput, calls=%fused_computation.36 | convolution fusion | flops 6444023808 | bytes 14680064 | tf_op jit(solution)/shard_map/dot_general | solution.py:32
  212.1 37.4 %reduce-scatter.15.cloned.1.call-done = bf16[3,64,2048]{2,1,0:T(8,128)(2,1)} async-done(((bf16[3,256,2048]{2,1,0:T(8,128)(2,1)}), bf16[3,64,2048]{2,1,0:T(8,128)(2,1)}) %reduce-scatter.15.cloned.1.call-update) | async-done | bytes 786448 | tf_op jit(solution)/shard_map/reduce_scatter | solution.py:96
  255.4 28.6 %all-gather.11.cloned.1.call-done = bf16[3,256,2048]{2,1,0:T(8,128)(2,1)} async-done(((bf16[3,64,2048]{2,1,0:T(8,128)(2,1)}), bf16[3,256,2048]{2,1,0:T(8,128)(2,1)}) %all-gather.11.cloned.1.call-update) | async-done | bytes 3145744 | tf_op jit(solution)/shard_map/all_gather | solution.py:93
  291.6 8.0 bitcast_convert_fusion
  299.6 6.4 fusion
  306.1 6.6 fusion.2
  321.2 30.9 %reduce-scatter.19.cloned.1.call-done = bf16[3,256,256]{1,2,0:T(8,128)(2,1)} async-done(((bf16[3,1024,256]{1,2,0:T(8,128)(2,1)}), bf16[3,256,256]{1,2,0:T(8,128)(2,1)}) %reduce-scatter.19.cloned.1.call-update) | async-done | bytes 393232 | tf_op jit(solution)/shard_map/reduce_scatter | solution.py:187
  359.4 11.9 %convolution_convert_fusion.3 = bf16[768,2048]{1,0:T(8,128)(2,1)} fusion(bf16[768,2048]{1,0:T(8,128)(2,1)} %get-tuple-element.35, bf16[2048,2048]{1,0:T(8,128)(2,1)} %param.32), kind=kOutput, calls=%fused_computation.37 | convolution fusion | flops 6444023808 | bytes 14680064 | tf_op jit(solution)/shard_map/dot_general | solution.py:163
  373.3 7.8 convolution_convert_fusion.1
  394.7 33.1 %reduce-scatter.17.cloned.1.call-done = bf16[3,64,2048]{2,1,0:T(8,128)(2,1)} async-done(((bf16[3,256,2048]{2,1,0:T(8,128)(2,1)}), bf16[3,64,2048]{2,1,0:T(8,128)(2,1)}) %reduce-scatter.17.cloned.1.call-update) | async-done | bytes 786448 | tf_op jit(solution)/shard_map/reduce_scatter | solution.py:96
  431.8 36.2 %reduce-scatter.13.cloned.1.call-done = bf16[3,64,2048]{2,1,0:T(8,128)(2,1)} async-done(((bf16[3,256,2048]{2,1,0:T(8,128)(2,1)}), bf16[3,64,2048]{2,1,0:T(8,128)(2,1)}) %reduce-scatter.13.cloned.1.call-update) | async-done | bytes 786448 | tf_op jit(solution)/shard_map/reduce_scatter | solution.py:96
  475.5 9.1 %add_convert_fusion.1 = bf16[1024,2048]{1,0:T(8,128)(2,1)} fusion(bf16[1024,2048]{1,0:T(8,128)(2,1)} %collective-permute-done.2, bf16[768,2048]{1,0:T(8,128)(2,1)} %copy-done.36, bf16[768,2048]{1,0:T(8,128)(2,1)} %bitcast.170, s32[]{:T(128)S(6)} %select_n.13), kind=kOutput, calls=%fused_computation.14 | convolution fusion | flops 3227516928 | bytes 13107204 | tf_op jit(solution)/shard_map/dot_general | solution.py:28
  484.8 6.0 convolution_convert_fusion
  492.4 90.7 %collective-permute-done.3 = bf16[2048,1024]{1,0:T(8,128)(2,1)S(1)} collective-permute-done((bf16[2048,1024]{1,0:T(8,128)(2,1)S(1)}, bf16[2048,1024]{1,0:T(8,128)(2,1)S(1)}, u32[]{:S(2)}, u32[]{:S(2)}) %collective-permute-start.3) | collective-permute-done | bytes 4194336 | tf_op jit(solution)/shard_map/ppermute | solution.py:42
  583.0 5.2 add_convert_fusion
  593.5 22.4 %collective-permute-done.1 = bf16[512,1024]{1,0:T(8,128)(2,1)S(1)} collective-permute-done((bf16[512,1024]{1,0:T(8,128)(2,1)S(1)}, bf16[512,1024]{1,0:T(8,128)(2,1)S(1)}, u32[]{:S(2)}, u32[]{:S(2)}) %collective-permute-start.1) | collective-permute-done | bytes 1048608 | tf_op jit(solution)/shard_map/ppermute | solution.py:42
  622.2 21.6 %collective-permute-done = bf16[1024,512]{1,0:T(8,128)(2,1)S(1)} collective-permute-done((bf16[1024,512]{1,0:T(8,128)(2,1)S(1)}, bf16[1024,512]{1,0:T(8,128)(2,1)S(1)}, u32[]{:S(2)}, u32[]{:S(2)}) %collective-permute-start) | collective-permute-done | bytes 1048608 | tf_op jit(solution)/shard_map/ppermute | solution.py:42
  651.6 13.7 %reduce-scatter.29.cloned.1.call-done = bf16[2048,256]{1,0:T(8,128)(2,1)} async-done(((bf16[2048,1024]{1,0:T(8,128)(2,1)}), bf16[2048,256]{1,0:T(8,128)(2,1)}) %reduce-scatter.29.cloned.1.call-update) | async-done | bytes 1048592 | tf_op jit(solution)/shard_map/reduce_scatter | solution.py:51
  668.0 27.3 %reduce-scatter.25.cloned.1.call-done = bf16[512,256]{1,0:T(8,128)(2,1)} async-done(((bf16[512,1024]{1,0:T(8,128)(2,1)}), bf16[512,256]{1,0:T(8,128)(2,1)}) %reduce-scatter.25.cloned.1.call-update) | async-done | bytes 262160 | tf_op jit(solution)/shard_map/reduce_scatter | solution.py:51
  697.1 26.2 %reduce-scatter.21.cloned.1.call-done = bf16[256,512]{1,0:T(8,128)(2,1)} async-done(((bf16[1024,512]{1,0:T(8,128)(2,1)}), bf16[256,512]{1,0:T(8,128)(2,1)}) %reduce-scatter.21.cloned.1.call-update) | async-done | bytes 262160 | tf_op jit(solution)/shard_map/reduce_scatter | solution.py:51
  725.1 71.0 %all-reduce.8.cloned.1.call-done = bf16[8,17092]{1,0:T(8,128)(2,1)} async-done(((bf16[8,17092]{1,0:T(8,128)(2,1)}), bf16[8,17092]{1,0:T(8,128)(2,1)}) %all-reduce.8.cloned.1.call-update) | async-done | bytes 273488
  (216 shorter events, 115.7 us)
Async XLA Ops:
  7.2 73.4 %copy-start = (bf16[512,2048]{1,0:T(8,128)(2,1)S(1)}, bf16[512,2048]{1,0:T(8,128)(2,1)}, u32[]{:S(2)}) copy-start(bf16[512,2048]{1,0:T(8,128)(2,1)} %param.26) | copy-start | bytes 6291460
  7.2 49.2 %all-gather.5.cloned.1.call-start = ((), (), s32[]{:S(2)}) async-start(), calls=%async_computation.10 | async-start | bytes 1966080 | tf_op jit(solution)/shard_map/all_gather | solution.py:117
  16.5 105.4 %reduce-scatter.11.cloned.1.call-start = ((), (), s32[]{:S(2)}) async-start(), calls=%async_computation.11 | async-start | bytes 3932160 | tf_op jit(solution)/shard_map/reduce_scatter | solution.py:96
  85.2 69.8 %all-gather.7.cloned.1.call-start = ((), (), s32[]{:S(2)}) async-start(), calls=%async_computation.12 | async-start | bytes 3932160 | tf_op jit(solution)/shard_map/all_gather | solution.py:93
  126.3 59.2 %all-gather.9.cloned.1.call-start = ((), (), s32[]{:S(2)}) async-start(), calls=%async_computation.14 | async-start | bytes 3932160 | tf_op jit(solution)/shard_map/all_gather | solution.py:93
  128.7 120.8 %reduce-scatter.15.cloned.1.call-start = ((), (), s32[]{:S(2)}) async-start(), calls=%async_computation.15 | async-start | bytes 3932160 | tf_op jit(solution)/shard_map/reduce_scatter | solution.py:96
  211.7 72.4 %all-gather.11.cloned.1.call-start = ((), (), s32[]{:S(2)}) async-start(), calls=%async_computation.16 | async-start | bytes 3932160 | tf_op jit(solution)/shard_map/all_gather | solution.py:93
  255.4 96.8 %reduce-scatter.19.cloned.1.call-start = ((), (), s32[]{:S(2)}) async-start(), calls=%async_computation.18 | async-start | bytes 1966080 | tf_op jit(solution)/shard_map/reduce_scatter | solution.py:187
  316.5 70.8 %all-reduce.6.cloned.1.call-start = ((), (), s32[]{:S(2)}) async-start(), calls=%async_computation.24 | async-start | bytes 1048576
  321.2 38.1 %copy-start.17 = (bf16[3,256,4,128]{3,2,1,0:T(4,128)(2,1)}, bf16[3,256,4,128]{3,2,1,0:T(4,128)(2,1)S(1)}, u32[]{:S(2)}) copy-start(bf16[3,256,4,128]{3,2,1,0:T(4,128)(2,1)S(1)} %copy.87) | copy-start | bytes 2359300
  354.2 73.6 %reduce-scatter.17.cloned.1.call-start = ((), (), s32[]{:S(2)}) async-start(), calls=%async_computation.17 | async-start | bytes 3932160 | tf_op jit(solution)/shard_map/reduce_scatter | solution.py:96
  359.3 108.6 %reduce-scatter.13.cloned.1.call-start = ((), (), s32[]{:S(2)}) async-start(), calls=%async_computation.13 | async-start | bytes 3932160 | tf_op jit(solution)/shard_map/reduce_scatter | solution.py:96
  371.3 274.9 %reduce-scatter.23.cloned.1.call-start = ((), (), s32[]{:S(2)}) async-start(), calls=%async_computation.20 | async-start | bytes 1351680 | tf_op jit(solution)/shard_map/reduce_scatter | solution.py:211
  381.1 94.3 %collective-permute-start.2 = (bf16[1024,2048]{1,0:T(8,128)(2,1)}, bf16[1024,2048]{1,0:T(8,128)(2,1)}, u32[]{:S(2)}, u32[]{:S(2)}) collective-permute-start(bf16[1024,2048]{1,0:T(8,128)(2,1)} %convolution_convert_fusion.1), channel_id=1, source_target_pairs={{0,16},{16,0},{1,17},{17,1},{2,18},{18,2},{3,19},{19,3},{4,20},{20... | collective-permute-start | bytes 12582920 | tf_op jit(solution)/shard_map/ppermute | solution.py:42
  388.3 39.5 %copy-start.20 = (f32[2048]{0:T(1024)S(1)}, f32[2048]{0:T(1024)}, u32[]{:S(2)}) copy-start(f32[2048]{0:T(1024)} %copy-done.19) | copy-start | bytes 24580
  391.6 76.4 %copy-start.4 = (f32[3,64,2048]{2,1,0:T(8,128)S(1)}, f32[3,64,2048]{2,1,0:T(8,128)}, u32[]{:S(2)}) copy-start(f32[3,64,2048]{2,1,0:T(8,128)} %copy-done.2) | copy-start | bytes 4718596
  391.6 76.4 %copy-start.7 = (bf16[3,64,2048]{2,1,0:T(8,128)(2,1)S(1)}, bf16[3,64,2048]{2,1,0:T(8,128)(2,1)}, u32[]{:S(2)}) copy-start(bf16[3,64,2048]{2,1,0:T(8,128)(2,1)} %param.19) | copy-start | bytes 2359300
  475.4 173.2 %reduce-scatter.27.cloned.1.call-start = ((), (), s32[]{:S(2)}) async-start(), calls=%async_computation.22 | async-start | bytes 5242880 | tf_op jit(solution)/shard_map/reduce_scatter | solution.py:51
  484.6 180.8 %reduce-scatter.29.cloned.1.call-start = ((), (), s32[]{:S(2)}) async-start(), calls=%async_computation.23 | async-start | bytes 5242880 | tf_op jit(solution)/shard_map/reduce_scatter | solution.py:51
  484.8 98.2 %copy-start.32 = (bf16[3,256,2048]{2,1,0:T(8,128)(2,1)S(1)}, bf16[3,256,2048]{2,1,0:T(8,128)(2,1)}, u32[]{:S(2)}) copy-start(bf16[3,256,2048]{2,1,0:T(8,128)(2,1)} %all-gather.9.cloned.1.call-done) | copy-start | bytes 9437188
  484.8 98.2 %copy-start.37 = (bf16[768,2048]{1,0:T(8,128)(2,1)S(1)}, bf16[768,2048]{1,0:T(8,128)(2,1)}, u32[]{:S(2)}) copy-start(bf16[768,2048]{1,0:T(8,128)(2,1)} %get-tuple-element.35) | copy-start | bytes 9437188
  490.8 92.2 %collective-permute-start.3 = (bf16[2048,1024]{1,0:T(8,128)(2,1)S(1)}, bf16[2048,1024]{1,0:T(8,128)(2,1)S(1)}, u32[]{:S(2)}, u32[]{:S(2)}) collective-permute-start(bf16[2048,1024]{1,0:T(8,128)(2,1)S(1)} %convolution_convert_fusion), channel_id=1, source_target_pairs={{0,16},{16,0},{1,17},{17,1},{2,18},{18,2},{3,19},{19,3},{4,20},{20... | collective-permute-start | bytes 12582920 | tf_op jit(solution)/shard_map/ppermute | solution.py:42
  588.3 107.0 %reduce-scatter.25.cloned.1.call-start = ((), (), s32[]{:S(2)}) async-start(), calls=%async_computation.21 | async-start | bytes 1310720 | tf_op jit(solution)/shard_map/reduce_scatter | solution.py:51
  589.4 26.5 %copy-start.16 = (bf16[3,256,2048]{2,1,0:T(8,128)(2,1)S(1)}, bf16[3,256,2048]{2,1,0:T(8,128)(2,1)}, u32[]{:S(2)}) copy-start(bf16[3,256,2048]{2,1,0:T(8,128)(2,1)} %all-gather.11.cloned.1.call-done) | copy-start | bytes 9437188
  592.0 26.0 %copy-start.18 = (bf16[3,256,4,128]{3,2,1,0:T(4,128)(2,1)S(1)}, bf16[3,256,4,128]{3,2,1,0:T(4,128)(2,1)}, u32[]{:S(2)}) copy-start(bf16[3,256,4,128]{3,2,1,0:T(4,128)(2,1)} %copy-done.17) | copy-start | bytes 2359300
  592.0 23.9 %collective-permute-start.1 = (bf16[512,1024]{1,0:T(8,128)(2,1)S(1)}, bf16[512,1024]{1,0:T(8,128)(2,1)S(1)}, u32[]{:S(2)}, u32[]{:S(2)}) collective-permute-start(bf16[512,1024]{1,0:T(8,128)(2,1)S(1)} %fusion.50), channel_id=1, source_target_pairs={{0,16},{16,0},{1,17},{17,1},{2,18},{18,2},{3,19},{19,3},{4,20},{20... | collective-permute-start | bytes 3145736 | tf_op jit(solution)/shard_map/ppermute | solution.py:42
  617.9 105.3 %reduce-scatter.21.cloned.1.call-start = ((), (), s32[]{:S(2)}) async-start(), calls=%async_computation.19 | async-start | bytes 1310720 | tf_op jit(solution)/shard_map/reduce_scatter | solution.py:51
  618.0 25.8 %copy-start.14 = (bf16[3,256,2048]{2,1,0:T(8,128)(2,1)S(1)}, bf16[3,256,2048]{2,1,0:T(8,128)(2,1)}, u32[]{:S(2)}) copy-start(bf16[3,256,2048]{2,1,0:T(8,128)(2,1)} %copy-done.13) | copy-start | bytes 9437188
  620.6 27.5 %copy-start.34 = (u32[32]{0:T(128)S(1)}, u32[32]{0:T(128)}, u32[]{:S(2)}) copy-start(u32[32]{0:T(128)} %constant.83) | copy-start | bytes 388
  620.6 23.2 %collective-permute-start = (bf16[1024,512]{1,0:T(8,128)(2,1)S(1)}, bf16[1024,512]{1,0:T(8,128)(2,1)S(1)}, u32[]{:S(2)}, u32[]{:S(2)}) collective-permute-start(bf16[1024,512]{1,0:T(8,128)(2,1)S(1)} %multiply_convert_fusion.2), channel_id=1, source_target_pairs={{0,16},{16,0},{1,17},{17,1},{2,18},{18,2},{3,19},{19,3},{4,20},{20... | collective-permute-start | bytes 3145736 | tf_op jit(solution)/shard_map/ppermute | solution.py:42
  645.8 150.3 %all-reduce.8.cloned.1.call-start = ((), (), s32[]{:S(2)}) async-start(), calls=%async_computation.25 | async-start | bytes 548864
  648.7 152.7 %copy-start.1 = (bf16[512,2048]{1,0:T(8,128)(2,1)S(1)}, bf16[512,2048]{1,0:T(8,128)(2,1)}, u32[]{:S(2)}) copy-start(bf16[512,2048]{1,0:T(8,128)(2,1)} %param.26) | copy-start | bytes 6291460
  (26 other events, 105.3 us)
Sparse Core Ops, SparseCore 0:
  16.6 39.7 all-gather.4
  85.3 36.5 reduce-scatter.10
  126.4 28.4 all-gather.6
  157.0 28.4 all-gather.8
  211.8 37.7 reduce-scatter.14
  255.5 28.5 all-gather.10
  316.7 35.4 reduce-scatter.18
  355.1 32.2 all-reduce.5
  389.9 37.8 reduce-scatter.16
  430.2 37.7 reduce-scatter.12
  475.5 25.0 reduce-scatter.22
  502.7 76.7 reduce-scatter.26
  588.4 76.8 reduce-scatter.28
  667.5 27.7 reduce-scatter.24
  697.4 25.7 reduce-scatter.20
  726.5 69.5 all-reduce.7
where the time goes:
time: 812 us; the launch traced here: 808 us
  waiting for transfers between devices  548 us (67%)
  matrix products  152 us (19%)
  other arithmetic  57.5 us (7%)
  local copies, waits for them, and re-layouts  27.4 us (3%)
  between operations  15.5 us (2%)
  starting transfers between devices  8.25 us (1%)
    reduce_scatter x4, waiting for transfers between devices, scatter_own(): lax.psum_scatter(values_in.astype(BF16).reshape(n_rows, seq_len, model_wi...  138 us
    ppermute x4, waiting for transfers between devices, dp_exchange(): arrived.append(lax.ppermute(part_for(target).astype(BF16), 'dp', pairs))  135 us
    unnamed x18, waiting for transfers between devices  75.8 us
    all_gather x3, waiting for transfers between devices, gather_own(): return lax.all_gather(values_in, 'tensor', axis=1, tiled=True)  70.9 us
    reduce_scatter x4, waiting for transfers between devices, two_stage(): lax.psum_scatter(total.astype(BF16), 'seq', scatter_dimension=dim, tiled=...  67.2 us
    dot_general x5, matrix products, times_transposed(): lax.dot_general(left_in, right_in, (((1,), (1,)), ((), ())), preferred_el...  39.6 us
    dot_general x9, matrix products, across_rows(): lax.dot_general(left_in, right_in, (((0,), (0,)), ((), ())), preferred_el...  38.9 us
    reduce_scatter x1, waiting for transfers between devices, shards(): lax.psum_scatter(grad_kv.astype(BF16), 'seq', scatter_dimension=1, tiled=...  30.9 us
  transfers between devices with their start and end apart: 20, of which 17 were waited for; matrix products, arithmetic and copies ran while one was open for 15% of the time, Pallas kernels for 0%

commit v1 on v0

--- a/solution.py
+++ b/solution.py
@@ -90,7 +90,9 @@
         return lax.dynamic_slice_in_dim(values_in, tensor_index * share_len, share_len, 1)
 
     def gather_own(values_in):
-        return lax.all_gather(values_in, "tensor", axis=1, tiled=True)
+        return jnp.concatenate(
+            lax.all_to_all(jnp.stack([values_in] * lax.axis_size("tensor")), "tensor", 0, 0), axis=1
+        )
 
     def scatter_own(values_in):
         return lax.psum_scatter(

time: 812 us -> 932 us (1.15)
  waiting for transfers between devices: 548 us -> 643 us
  local copies, waits for them, and re-layouts: 27.4 us -> 44 us
  starting transfers between devices: 8.25 us -> 21.4 us
    ppermute x4, waiting for transfers between devices: 135 us -> 210 us  [dp_exchange(): arrived.append(lax.ppermute(part_for(target).astype(BF16), 'dp', pairs))]
    all_to_all x0 -> x3, waiting for transfers between devices: none -> 73.1 us  [gather_own(): lax.all_to_all(jnp.stack([values_in] * lax.axis_size('tensor')), 'tensor'...]
    all_gather x3 -> x0, waiting for transfers between devices: 70.9 us -> none  [gather_own(): return lax.all_gather(values_in, 'tensor', axis=1, tiled=True)]
    all_to_all x0 -> x3, starting transfers between devices: none -> 14.3 us  [gather_own(): lax.all_to_all(jnp.stack([values_in] * lax.axis_size('tensor')), 'tensor'...]
    unnamed x18 -> x15, waiting for transfers between devices: 75.8 us -> 86.1 us
  transfers between devices with their start and end apart: 20 -> 20, of which waited for: 17 -> 15; matrix products, arithmetic and copies ran while one was open for 15% -> 12% of each run, Pallas kernels for 0% -> 0%
where the time goes in v1:
time: 932 us; the launch traced here: 928 us
  waiting for transfers between devices  643 us (69%)
  matrix products  147 us (16%)
  other arithmetic  56.1 us (6%)
  local copies, waits for them, and re-layouts  44 us (5%)
  starting transfers between devices  21.4 us (2%)
  between operations  15.5 us (2%)
    ppermute x4, waiting for transfers between devices, dp_exchange(): arrived.append(lax.ppermute(part_for(target).astype(BF16), 'dp', pairs))  210 us
    reduce_scatter x4, waiting for transfers between devices, scatter_own(): lax.psum_scatter(values_in.astype(BF16).reshape(n_rows, seq_len, model_wi...  145 us
    unnamed x15, waiting for transfers between devices  86.1 us
    all_to_all x3, waiting for transfers between devices, gather_own(): lax.all_to_all(jnp.stack([values_in] * lax.axis_size('tensor')), 'tensor'...  73.1 us
    reduce_scatter x4, waiting for transfers between devices, two_stage(): lax.psum_scatter(total.astype(BF16), 'seq', scatter_dimension=dim, tiled=...  67.6 us
    dot_general x9, matrix products, across_rows(): lax.dot_general(left_in, right_in, (((0,), (0,)), ((), ())), preferred_el...  39.5 us
    dot_general x5, matrix products, times_transposed(): lax.dot_general(left_in, right_in, (((1,), (1,)), ((), ())), preferred_el...  35.1 us
    reduce_scatter x1, waiting for transfers between devices, shards(): lax.psum_scatter(grad_kv.astype(BF16), 'seq', scatter_dimension=1, tiled=...  30.7 us
  transfers between devices with their start and end apart: 20, of which 15 were waited for; matrix products, arithmetic and copies ran while one was open for 12% of the time, Pallas kernels for 0%

profile of v1, /device:TPU:0, one launch (start us, length us, event | category | flops | bytes accessed | tf_op | source)
XLA Modules:
  0.0 927.9 jit_solution(11268964785166369088)
XLA Ops:
  16.9 5.2 multiply_convert_fusion.4
  25.9 30.5 %all-gather.2.cloned.1.call-done = bf16[3,1024,256]{2,1,0:T(8,128)(2,1)} async-done(((bf16[3,256,256]{2,1,0:T(8,128)(2,1)}), bf16[3,1024,256]{2,1,0:T(8,128)(2,1)}) %all-gather.2.cloned.1.call-update) | async-done | bytes 1572880 | tf_op jit(solution)/shard_map/all_gather | solution.py:119
  56.4 7.7 fusion.4
  64.2 7.0 fusion.3
  71.1 7.3 fusion.55
  93.8 5.5 convert_element_type.180
  99.3 40.0 %reduce-scatter.11.cloned.1.call-done = bf16[3,64,2048]{2,1,0:T(8,128)(2,1)} async-done(((bf16[3,256,2048]{2,1,0:T(8,128)(2,1)}), bf16[3,64,2048]{2,1,0:T(8,128)(2,1)}) %reduce-scatter.11.cloned.1.call-update) | async-done | bytes 786448 | tf_op jit(solution)/shard_map/reduce_scatter | solution.py:98
  160.2 32.3 %all-to-all-done = bf16[4,3,64,2048]{3,2,1,0:T(8,128)(2,1)} async-done(((bf16[4,3,64,2048]{3,2,1,0:T(8,128)(2,1)}), bf16[4,3,64,2048]{3,2,1,0:T(8,128)(2,1)}, u32[]{:S(2)}, u32[]{:S(2)}) %all-to-all-start) | async-done | bytes 3145760 | tf_op jit(solution)/shard_map/all_to_all | solution.py:94
  194.7 13.6 %multiply_convert_fusion.1 = (bf16[768,2048]{1,0:T(8,128)(2,1)}, f32[768,2048]{1,0:T(8,128)}) fusion(f32[2048]{0:T(1024)S(1)} %convert_element_type.196, bf16[768,2048]{1,0:T(8,128)(2,1)S(1)} %bitcast.154, bf16[2048,2048]{1,0:T(8,128)(2,1)} %param.30), kind=kOutput, calls=%fused_computation.26 | convolution fusion | flops 6458179584 | bytes 20979712 | tf_op jit(solution)/shard_map/dot_general | solution.py:149
  208.3 15.2 %fusion.85 = (bf16[2048]{0:T(1024)(128)(2,1)S(1)}, bf16[768,2048]{1,0:T(8,128)(2,1)S(1)}) fusion(f32[768,2048]{1,0:T(8,128)} %get-tuple-element.36, f32[2048]{0:T(1024)S(1)} %convert_element_type.196, bf16[768,2048]{1,0:T(8,128)(2,1)S(1)} %bitcast.152, bf16[2048,2048]{1,0:T(8,128)(2,1)} %param.32), kind=kOutput, calls=%fused_computation.154 | convolution fusion | flops 6477051904 | bytes 20983808 | tf_op jit(solution)/shard_map/dot_general | solution.py:32
  223.6 8.3 convolution_convert_fusion.2
  231.9 35.8 %reduce-scatter.15.cloned.1.call-done = bf16[3,64,2048]{2,1,0:T(8,128)(2,1)} async-done(((bf16[3,256,2048]{2,1,0:T(8,128)(2,1)}), bf16[3,64,2048]{2,1,0:T(8,128)(2,1)}) %reduce-scatter.15.cloned.1.call-update) | async-done | bytes 786448 | tf_op jit(solution)/shard_map/reduce_scatter | solution.py:98
  279.5 36.9 %all-to-all-done.2 = bf16[4,3,64,2048]{3,2,1,0:T(8,128)(2,1)} async-done(((bf16[4,3,64,2048]{3,2,1,0:T(8,128)(2,1)}), bf16[4,3,64,2048]{3,2,1,0:T(8,128)(2,1)}, u32[]{:S(2)}, u32[]{:S(2)}) %all-to-all-start.2) | async-done | bytes 3145760 | tf_op jit(solution)/shard_map/all_to_all | solution.py:94
  326.0 8.0 bitcast_convert_fusion
  334.0 6.4 fusion
  340.5 6.6 fusion.2
  355.9 30.7 %reduce-scatter.19.cloned.1.call-done = bf16[3,256,256]{1,2,0:T(8,128)(2,1)} async-done(((bf16[3,1024,256]{1,2,0:T(8,128)(2,1)}), bf16[3,256,256]{1,2,0:T(8,128)(2,1)}) %reduce-scatter.19.cloned.1.call-update) | async-done | bytes 393232 | tf_op jit(solution)/shard_map/reduce_scatter | solution.py:189
  388.7 5.1 multiply_convert_fusion
  393.9 11.9 %convolution_convert_fusion.3 = bf16[768,2048]{1,0:T(8,128)(2,1)} fusion(bf16[768,2048]{1,0:T(8,128)(2,1)} %get-tuple-element.35, bf16[2048,2048]{1,0:T(8,128)(2,1)} %param.32), kind=kOutput, calls=%fused_computation.37 | convolution fusion | flops 6444023808 | bytes 14680064 | tf_op jit(solution)/shard_map/dot_general | solution.py:165
  408.0 13.6 %all-reduce.6.cloned.1.call-done = bf16[3,256,256]{2,0,1:T(4,128)(2,1)} async-done(((bf16[3,256,256]{2,0,1:T(4,128)(2,1)}), bf16[3,256,256]{2,0,1:T(4,128)(2,1)}) %all-reduce.6.cloned.1.call-update) | async-done | bytes 393232
  429.0 33.0 %reduce-scatter.17.cloned.1.call-done = bf16[3,64,2048]{2,1,0:T(8,128)(2,1)} async-done(((bf16[3,256,2048]{2,1,0:T(8,128)(2,1)}), bf16[3,64,2048]{2,1,0:T(8,128)(2,1)}) %reduce-scatter.17.cloned.1.call-update) | async-done | bytes 786448 | tf_op jit(solution)/shard_map/reduce_scatter | solution.py:98
  466.0 36.3 %reduce-scatter.13.cloned.1.call-done = bf16[3,64,2048]{2,1,0:T(8,128)(2,1)} async-done(((bf16[3,256,2048]{2,1,0:T(8,128)(2,1)}), bf16[3,64,2048]{2,1,0:T(8,128)(2,1)}) %reduce-scatter.13.cloned.1.call-update) | async-done | bytes 786448 | tf_op jit(solution)/shard_map/reduce_scatter | solution.py:98
  502.3 4.8 multiply_add_fusion
  514.3 6.7 convolution_convert_fusion.1
  521.4 17.6 %collective-permute-done.1 = bf16[512,1024]{1,0:T(8,128)(2,1)} collective-permute-done((bf16[512,1024]{1,0:T(8,128)(2,1)S(1)}, bf16[512,1024]{1,0:T(8,128)(2,1)}, u32[]{:S(2)}, u32[]{:S(2)}) %collective-permute-start.1) | collective-permute-done | bytes 1048608 | tf_op jit(solution)/shard_map/ppermute | solution.py:42
  547.0 103.0 %collective-permute-done = bf16[1024,512]{1,0:T(8,128)(2,1)S(1)} collective-permute-done((bf16[1024,512]{1,0:T(8,128)(2,1)S(1)}, bf16[1024,512]{1,0:T(8,128)(2,1)S(1)}, u32[]{:S(2)}, u32[]{:S(2)}) %collective-permute-start) | collective-permute-done | bytes 1048608 | tf_op jit(solution)/shard_map/ppermute | solution.py:42
  652.0 9.0 add_convert_fusion.1
  661.3 6.0 convolution_convert_fusion
  668.8 89.8 %collective-permute-done.3 = bf16[2048,1024]{1,0:T(8,128)(2,1)S(1)} collective-permute-done((bf16[2048,1024]{1,0:T(8,128)(2,1)S(1)}, bf16[2048,1024]{1,0:T(8,128)(2,1)S(1)}, u32[]{:S(2)}, u32[]{:S(2)}) %collective-permute-start.3) | collective-permute-done | bytes 4194336 | tf_op jit(solution)/shard_map/ppermute | solution.py:42
  758.6 5.3 add_convert_fusion
  773.4 67.6 %reduce-scatter.29.cloned.1.call-done = bf16[2048,256]{1,0:T(8,128)(2,1)} async-done(((bf16[2048,1024]{1,0:T(8,128)(2,1)}), bf16[2048,256]{1,0:T(8,128)(2,1)}) %reduce-scatter.29.cloned.1.call-update) | async-done | bytes 1048592 | tf_op jit(solution)/shard_map/reduce_scatter | solution.py:51
  843.7 72.3 %all-reduce.8.cloned.1.call-done = bf16[8,17092]{1,0:T(8,128)(2,1)} async-done(((bf16[8,17092]{1,0:T(8,128)(2,1)}), bf16[8,17092]{1,0:T(8,128)(2,1)}) %all-reduce.8.cloned.1.call-update) | async-done | bytes 273488
  (230 shorter events, 133.5 us)
Async XLA Ops:
  7.2 73.5 %copy-start = (bf16[512,2048]{1,0:T(8,128)(2,1)S(1)}, bf16[512,2048]{1,0:T(8,128)(2,1)}, u32[]{:S(2)}) copy-start(bf16[512,2048]{1,0:T(8,128)(2,1)} %param.26) | copy-start | bytes 6291460
  7.2 49.2 %all-gather.2.cloned.1.call-start = ((), (), s32[]{:S(2)}) async-start(), calls=%async_computation.13 | async-start | bytes 1966080 | tf_op jit(solution)/shard_map/all_gather | solution.py:119
  16.5 122.8 %reduce-scatter.11.cloned.1.call-start = ((), (), s32[]{:S(2)}) async-start(), calls=%async_computation.14 | async-start | bytes 3932160 | tf_op jit(solution)/shard_map/reduce_scatter | solution.py:98
  88.9 58.6 %all-to-all-start.1 = ((bf16[4,3,64,2048]{3,2,1,0:T(8,128)(2,1)}), bf16[4,3,64,2048]{3,2,1,0:T(8,128)(2,1)}, u32[]{:S(2)}, u32[]{:S(2)}) async-start(bf16[4,3,64,2048]{3,2,1,0:T(8,128)(2,1)} %stack.21), calls=%async_computation.3 | async-start | bytes 6291456 | tf_op jit(solution)/shard_map/all_to_all | solution.py:94
  150.8 41.8 %all-to-all-start = ((bf16[4,3,64,2048]{3,2,1,0:T(8,128)(2,1)}), bf16[4,3,64,2048]{3,2,1,0:T(8,128)(2,1)}, u32[]{:S(2)}, u32[]{:S(2)}) async-start(bf16[4,3,64,2048]{3,2,1,0:T(8,128)(2,1)} %stack.20), calls=%async_computation.1 | async-start | bytes 6291456 | tf_op jit(solution)/shard_map/all_to_all | solution.py:94
  155.6 112.1 %reduce-scatter.15.cloned.1.call-start = ((), (), s32[]{:S(2)}) async-start(), calls=%async_computation.16 | async-start | bytes 3932160 | tf_op jit(solution)/shard_map/reduce_scatter | solution.py:98
  194.7 28.9 %slice-start = ((s8[8388608]{0:T(1024)(128)(4,1)}), s8[4194304]{0:T(1024)(128)(4,1)S(1)}, s32[]{:S(2)}) async-start(s8[8388608]{0:T(1024)(128)(4,1)} %bitcast.177), calls=%async_computation.26 | async-start | bytes 8388608
  208.3 15.3 %slice-start.1 = ((s8[8388608]{0:T(1024)(128)(4,1)}), s8[4194304]{0:T(1024)(128)(4,1)S(1)}, s32[]{:S(2)}) async-start(s8[8388608]{0:T(1024)(128)(4,1)} %bitcast.177), calls=%async_computation.27 | async-start | bytes 8388608
  274.7 41.6 %all-to-all-start.2 = ((bf16[4,3,64,2048]{3,2,1,0:T(8,128)(2,1)}), bf16[4,3,64,2048]{3,2,1,0:T(8,128)(2,1)}, u32[]{:S(2)}, u32[]{:S(2)}) async-start(bf16[4,3,64,2048]{3,2,1,0:T(8,128)(2,1)} %stack.44), calls=%async_computation.5 | async-start | bytes 6291456 | tf_op jit(solution)/shard_map/all_to_all | solution.py:94
  279.4 107.2 %reduce-scatter.19.cloned.1.call-start = ((), (), s32[]{:S(2)}) async-start(), calls=%async_computation.18 | async-start | bytes 1966080 | tf_op jit(solution)/shard_map/reduce_scatter | solution.py:189
  351.0 70.7 %all-reduce.6.cloned.1.call-start = ((), (), s32[]{:S(2)}) async-start(), calls=%async_computation.24 | async-start | bytes 1048576
  355.9 37.9 %copy-start.20 = (bf16[3,256,4,128]{3,2,1,0:T(4,128)(2,1)}, bf16[3,256,4,128]{3,2,1,0:T(4,128)(2,1)S(1)}, u32[]{:S(2)}) copy-start(bf16[3,256,4,128]{3,2,1,0:T(4,128)(2,1)S(1)} %copy.90) | copy-start | bytes 2359300
  388.7 73.3 %reduce-scatter.17.cloned.1.call-start = ((), (), s32[]{:S(2)}) async-start(), calls=%async_computation.17 | async-start | bytes 3932160 | tf_op jit(solution)/shard_map/reduce_scatter | solution.py:98
  393.8 108.4 %reduce-scatter.13.cloned.1.call-start = ((), (), s32[]{:S(2)}) async-start(), calls=%async_computation.15 | async-start | bytes 3932160 | tf_op jit(solution)/shard_map/reduce_scatter | solution.py:98
  405.8 358.6 %reduce-scatter.23.cloned.1.call-start = ((), (), s32[]{:S(2)}) async-start(), calls=%async_computation.20 | async-start | bytes 1351680 | tf_op jit(solution)/shard_map/reduce_scatter | solution.py:213
  422.6 39.3 %copy-start.23 = (f32[2048]{0:T(1024)S(1)}, f32[2048]{0:T(1024)}, u32[]{:S(2)}) copy-start(f32[2048]{0:T(1024)} %copy-done.22) | copy-start | bytes 24580
  425.9 76.4 %copy-start.4 = (f32[3,64,2048]{2,1,0:T(8,128)S(1)}, f32[3,64,2048]{2,1,0:T(8,128)}, u32[]{:S(2)}) copy-start(f32[3,64,2048]{2,1,0:T(8,128)} %copy-done.2) | copy-start | bytes 4718596
  425.9 76.4 %copy-start.7 = (bf16[3,64,2048]{2,1,0:T(8,128)(2,1)S(1)}, bf16[3,64,2048]{2,1,0:T(8,128)(2,1)}, u32[]{:S(2)}) copy-start(bf16[3,64,2048]{2,1,0:T(8,128)(2,1)} %param.19) | copy-start | bytes 2359300
  509.7 257.1 %reduce-scatter.25.cloned.1.call-start = ((), (), s32[]{:S(2)}) async-start(), calls=%async_computation.21 | async-start | bytes 1310720 | tf_op jit(solution)/shard_map/reduce_scatter | solution.py:51
  512.8 26.2 %collective-permute-start.1 = (bf16[512,1024]{1,0:T(8,128)(2,1)S(1)}, bf16[512,1024]{1,0:T(8,128)(2,1)}, u32[]{:S(2)}, u32[]{:S(2)}) collective-permute-start(bf16[512,1024]{1,0:T(8,128)(2,1)S(1)} %fusion.50), channel_id=1, source_target_pairs={{0,16},{16,0},{1,17},{17,1},{2,18},{18,2},{3,19},{19,3},{4,20},{20... | collective-permute-start | bytes 3145736 | tf_op jit(solution)/shard_map/ppermute | solution.py:42
  521.0 131.0 %collective-permute-start.2 = (bf16[1024,2048]{1,0:T(8,128)(2,1)}, bf16[1024,2048]{1,0:T(8,128)(2,1)}, u32[]{:S(2)}, u32[]{:S(2)}) collective-permute-start(bf16[1024,2048]{1,0:T(8,128)(2,1)} %convolution_convert_fusion.1), channel_id=1, source_target_pairs={{0,16},{16,0},{1,17},{17,1},{2,18},{18,2},{3,19},{19,3},{4,20},{20... | collective-permute-start | bytes 12582920 | tf_op jit(solution)/shard_map/ppermute | solution.py:42
  521.4 21.4 %copy-start.21 = (bf16[3,256,4,128]{3,2,1,0:T(4,128)(2,1)S(1)}, bf16[3,256,4,128]{3,2,1,0:T(4,128)(2,1)}, u32[]{:S(2)}) copy-start(bf16[3,256,4,128]{3,2,1,0:T(4,128)(2,1)} %copy-done.20) | copy-start | bytes 2359300
  542.8 225.8 %reduce-scatter.21.cloned.1.call-start = ((), (), s32[]{:S(2)}) async-start(), calls=%async_computation.19 | async-start | bytes 1310720 | tf_op jit(solution)/shard_map/reduce_scatter | solution.py:51
  542.8 107.1 %copy-start.18 = (bf16[3,256,2048]{2,1,0:T(8,128)(2,1)S(1)}, bf16[3,256,2048]{2,1,0:T(8,128)(2,1)}, u32[]{:S(2)}) copy-start(bf16[3,256,2048]{2,1,0:T(8,128)(2,1)} %copy-done.17) | copy-start | bytes 9437188
  545.4 104.5 %collective-permute-start = (bf16[1024,512]{1,0:T(8,128)(2,1)S(1)}, bf16[1024,512]{1,0:T(8,128)(2,1)S(1)}, u32[]{:S(2)}, u32[]{:S(2)}) collective-permute-start(bf16[1024,512]{1,0:T(8,128)(2,1)S(1)} %multiply_convert_fusion.2), channel_id=1, source_target_pairs={{0,16},{16,0},{1,17},{17,1},{2,18},{18,2},{3,19},{19,3},{4,20},{20... | collective-permute-start | bytes 3145736 | tf_op jit(solution)/shard_map/ppermute | solution.py:42
  651.9 118.6 %reduce-scatter.27.cloned.1.call-start = ((), (), s32[]{:S(2)}) async-start(), calls=%async_computation.22 | async-start | bytes 5242880 | tf_op jit(solution)/shard_map/reduce_scatter | solution.py:51
  661.1 179.9 %reduce-scatter.29.cloned.1.call-start = ((), (), s32[]{:S(2)}) async-start(), calls=%async_computation.23 | async-start | bytes 5242880 | tf_op jit(solution)/shard_map/reduce_scatter | solution.py:51
  661.3 97.4 %copy-start.14 = (bf16[4,3,64,2048]{3,2,0,1:T(8,128)(2,1)S(1)}, bf16[4,3,64,2048]{3,2,0,1:T(8,128)(2,1)}, u32[]{:S(2)}) copy-start(bf16[4,3,64,2048]{3,2,0,1:T(8,128)(2,1)} %copy.85) | copy-start | bytes 9437188
  661.3 97.3 %copy-start.40 = (bf16[768,2048]{1,0:T(8,128)(2,1)S(1)}, bf16[768,2048]{1,0:T(8,128)(2,1)}, u32[]{:S(2)}) copy-start(bf16[768,2048]{1,0:T(8,128)(2,1)} %get-tuple-element.35) | copy-start | bytes 9437188
  667.3 91.3 %collective-permute-start.3 = (bf16[2048,1024]{1,0:T(8,128)(2,1)S(1)}, bf16[2048,1024]{1,0:T(8,128)(2,1)S(1)}, u32[]{:S(2)}, u32[]{:S(2)}) collective-permute-start(bf16[2048,1024]{1,0:T(8,128)(2,1)S(1)} %convolution_convert_fusion), channel_id=1, source_target_pairs={{0,16},{16,0},{1,17},{17,1},{2,18},{18,2},{3,19},{19,3},{4,20},{20... | collective-permute-start | bytes 12582920 | tf_op jit(solution)/shard_map/ppermute | solution.py:42
  764.0 152.0 %all-reduce.8.cloned.1.call-start = ((), (), s32[]{:S(2)}) async-start(), calls=%async_computation.25 | async-start | bytes 548864
  768.6 152.6 %copy-start.1 = (bf16[512,2048]{1,0:T(8,128)(2,1)S(1)}, bf16[512,2048]{1,0:T(8,128)(2,1)}, u32[]{:S(2)}) copy-start(bf16[512,2048]{1,0:T(8,128)(2,1)} %param.26) | copy-start | bytes 6291460
  (31 other events, 140.1 us)
Sparse Core Ops, SparseCore 0:
  16.6 39.7 all-gather.1
  85.4 53.8 reduce-scatter.10
  232.0 35.6 reduce-scatter.14
  351.1 35.4 reduce-scatter.18
  389.4 32.2 all-reduce.5
  424.1 37.8 reduce-scatter.16
  464.5 37.7 reduce-scatter.12
  509.8 25.0 reduce-scatter.22
  542.9 27.2 reduce-scatter.24
  652.1 27.2 reduce-scatter.20
  681.7 75.3 reduce-scatter.26
  764.1 76.8 reduce-scatter.28
  844.3 71.5 all-reduce.7
